TPU v7x, 1024 devices: a whole 4x8x16 slice. The times are simulated.
1024 devices in a mesh: expert: 32 (over z, core), fsdp: 32 (over y, x).
Axes of the slice: x: 4, y: 8, z: 16, core: 2. Of those that a mesh axis runs over, the one named last changes fastest.
Arguments:
- tokens: bfloat16 [1024, 4096], P('expert', 'fsdp'), may hold values from -6 to 6
- expert_ids: int32 [1024, 8], P('expert'), may hold values from 0 to 63, all different within a row; in each aligned block of 32 rows (0 to 31, 32 to 63, ...) at most 8 rows name the same one
- gate_up: bfloat16 [64, 2, 1536, 4096], P('expert', None, 'fsdp'), may hold values from -0.09375 to 0.09375
- hidden_grad: bfloat16 [64, 1536, 256], P('expert', 'fsdp'), may hold values from -1.5 to 1.5
Outputs:
- hidden: bfloat16 [64, 1536, 256], P('expert', 'fsdp')
- gate_up_grad: bfloat16 [64, 2, 1536, 4096], P('expert', None, 'fsdp')
- tokens_grad: bfloat16 [1024, 4096], P('expert', 'fsdp')
Inputs may be any that keep to these rules, and one draw needn't show every extreme that they name: `expert_ids`: each token names 8 different experts. Among the 32 tokens of each aligned block (the tokens of one expert index) no expert is named by more than 8 tokens, and in some block one expert is named by exactly 8.
All inputs are finite; a program needn't handle non-finite values.
Results may differ from a plain program's by a relative error of at most 0.017.
Values may be sent and summed in bfloat16 or wider, within the bound.
No kernel may reach another device: no remote copies, remote signals or barrier semaphores. Data moves between devices by JAX's collectives and lax.ppermute only.
A program may use at most 64 MiB of HBM per device.

v0:
```python
import functools

import jax
import jax.numpy as jnp
from jax import lax
from jax.experimental import pallas as pl
from jax.experimental.pallas import tpu as pltpu
from jax.sharding import Mesh, PartitionSpec as P


LANES = 128
BF16 = jnp.bfloat16
F32 = jnp.float32
XN = 4


def dot(a, b, ca, cb):
    return lax.dot_general(a, b, (((ca,), (cb,)), ((), ())), preferred_element_type=F32)


def call(body, outs, flops, nbytes, *args, fetch=False):
    return pl.pallas_call(
        body,
        out_shape=[jax.ShapeDtypeStruct(s, d) for s, d in outs],
        in_specs=[
            pl.BlockSpec()
            if fetch
            else pl.BlockSpec(memory_space=pltpu.SMEM if a.ndim == 1 else pltpu.VMEM)
            for a in args
        ],
        out_specs=[pl.BlockSpec(memory_space=pltpu.VMEM) for _ in outs],
        cost_estimate=pl.CostEstimate(flops=flops, bytes_accessed=nbytes, transcendentals=0),
        compiler_params=pltpu.CompilerParams(vmem_limit_bytes=(60 if fetch else 20) << 20),
    )(*args)


def lanes(i):
    return slice(i * LANES, (i + 1) * LANES)


def swap(v, axis):
    return lax.all_to_all(v, axis, split_axis=0, concat_axis=0, tiled=True)


def lane_block(i):
    return pl.ds(pl.multiple_of(i * LANES, LANES), LANES)


def shift(v, axis, k):
    n = lax.axis_size(axis)
    return lax.ppermute(v, axis, [(i, (i + k) % n) for i in range(n)])


def gather_y(own):
    n = lax.axis_size("y")
    half = n // 2
    near = {0: own}
    up, down = own, own
    middle = own.shape[0] // 2
    for k in range(1, half):
        if k == half - 1:
            last = [(up[:middle], 2), (down[middle:], -2)]
        up, down = shift(up, "y", 1), shift(down, "y", -1)
        near[n - k], near[k] = up, down
    last = [shift(v, "y", k) for v, k in last]
    return [near[k] for k in range(n) if k != half] + last


def exchange_x(v1, v2, v3):
    from_left = shift(v1, "x", 1)
    from_right = shift(v3, "x", -1)
    return from_right, shift(v2, "x", 2), from_left


def split_body(at, w, *outs):
    for j, out in enumerate(outs):
        xj = lax.rem(at[0] + j, XN)
        for y in range(w.shape[1] // (XN * LANES)):
            out[:, lanes(y)] = w[:, lane_block(y * XN + xj)]


def join_body(at, *refs):
    out = refs[-1]
    for j, part in enumerate(refs[:-1]):
        xj = lax.rem(at[0] + j, XN)
        for y in range(part.shape[1] // LANES):
            out[:, lane_block(y * XN + xj)] = part[:, lanes(y)]


def forward_body(yn, at, at_y, *refs):
    chunks, last, refs = refs[: yn - 1], refs[yn - 1 : yn + 1], refs[yn + 1 :]
    weights, rows, sums = refs[:XN], refs[XN], refs[XN + 1]
    experts, half = rows.shape[0], yn // 2
    units = weights[0].shape[0] // experts
    for e in range(experts):
        for k in range(yn):
            where = lane_block(lax.rem(at_y[0] + k, yn))
            if k == half:
                rows[e, :, where] = last[2 * e // experts][e % (experts // 2)]
            else:
                rows[e, :, where] = chunks[k if k < half else k - 1][e]
        left = jnp.concatenate([w[e * units : (e + 1) * units] for w in weights], axis=0)
        total = dot(left, rows[e], 1, 1).astype(BF16)
        for j in range(XN):
            sums[lax.rem(at[0] + j, XN), e] = total[j * units : (j + 1) * units]


def gate_body(sums, hg, hidden, grads):
    half = hg.shape[1]
    for e in range(hg.shape[0]):
        total = sums[0, e].astype(F32)
        for x in range(1, XN):
            total = total + sums[x, e].astype(F32)
        gate, up = total[:half], total[half:]
        sig = 1.0 / (1.0 + jnp.exp(-gate))
        active = gate * sig
        g = hg[e].astype(F32)
        hidden[e] = (active * up).astype(BF16)
        gate_grad = (g * up * sig * (1.0 + gate * (1.0 - sig))).astype(BF16)
        up_grad = (g * active).astype(BF16)
        for x in range(grads.shape[0]):
            grads[x, e, :half] = gate_grad
            grads[x, e, half:] = up_grad


def backward_body(at, grads, *refs):
    weights, rows, part, wgrads = refs[:XN], refs[XN], refs[XN + 1], refs[XN + 2 :]
    experts, units = grads.shape[1], grads.shape[2]
    for e in range(experts):
        g = jnp.concatenate([grads[lax.rem(at[0] + j, XN), e] for j in range(XN)], axis=0)
        left = jnp.concatenate([w[e * units : (e + 1) * units] for w in weights], axis=0)
        back = dot(g, rows[e], 1, 0).astype(BF16)
        for j, out in enumerate(wgrads):
            out[e * units : (e + 1) * units] = back[j * units : (j + 1) * units]
        sent = dot(g, left, 0, 0).astype(BF16)
        for y in range(part.shape[0]):
            part[y, e] = sent[:, lanes(y)]


def pick_body(capacity, ids, tokens, rows, pick):
    count, block = ids.shape
    every = rows.shape[0]
    experts = every // capacity
    named = lax.broadcasted_iota(jnp.int32, (experts, block), 0)
    chosen = jnp.zeros((experts, block), F32)
    for k in range(count):
        chosen = chosen + jnp.where(ids[k : k + 1, :] == named, 1.0, 0.0)
    earlier = lax.broadcasted_iota(jnp.int32, (block, block), 0) < lax.broadcasted_iota(
        jnp.int32, (block, block), 1
    )
    chosen = chosen.astype(BF16)
    before = dot(chosen, jnp.where(earlier, 1.0, 0.0).astype(BF16), 1, 0).astype(BF16)
    slot = lax.broadcasted_iota(jnp.int32, (every, experts), 0)
    expert = lax.broadcasted_iota(jnp.int32, (every, experts), 1)
    spread = jnp.where(lax.div(slot, capacity) == expert, 1.0, 0.0).astype(BF16)
    place = lax.rem(lax.broadcasted_iota(jnp.int32, (every, block), 0), capacity).astype(F32)
    here = (dot(spread, chosen, 1, 0) > 0.5) & (dot(spread, before, 1, 0) == place)
    matrix = jnp.where(here, 1.0, 0.0).astype(BF16)
    pick[...] = matrix
    rows[...] = dot(matrix, tokens[...], 1, 0).astype(BF16)


def fold_body(pick, rows, out):
    out[...] = dot(pick[...], rows[...], 0, 0).astype(BF16)


def sum_body(parts, out):
    capacity = out.shape[2]
    for e in range(out.shape[1]):
        total = parts[0, e].astype(F32)
        for y in range(1, parts.shape[0]):
            total = total + parts[y, e].astype(F32)
        for g in range(out.shape[0]):
            out[g, e] = total[g * capacity : (g + 1) * capacity].astype(BF16)


def body(tokens, expert_ids, gate_up, hidden_grad):
    groups = lax.axis_size("expert")
    yn = lax.axis_size("y")
    experts, _, units, width = gate_up.shape
    rows_w = experts * 2 * units
    slots = hidden_grad.shape[2]
    capacity = slots // groups
    quarter = width // XN

    at = lax.axis_index("x").astype(jnp.int32)[None]
    at_y = lax.axis_index("y").astype(jnp.int32)[None]

    flat = gate_up.reshape(rows_w, width)
    w0, o1, o2, o3 = call(
        split_body, [((rows_w, quarter), BF16)] * XN, 0, 4 * rows_w * width, at, flat
    )
    weights = (w0,) + exchange_x(o1, o2, o3)

    ids = jnp.transpose(expert_ids)
    every = experts * slots
    outgoing, pick = call(
        functools.partial(pick_body, capacity),
        [((every, LANES), BF16), ((every, ids.shape[1]), BF16)],
        1 << 22, 1 << 18, ids, tokens, fetch=True,
    )
    arrived = swap(outgoing.reshape(groups, experts, capacity, LANES), "expert")
    own = jnp.transpose(arrived, (1, 0, 2, 3)).reshape(experts, slots, LANES)
    chunks = gather_y(own)

    flops = 2 * 4 * rows_w * quarter * slots
    rows, sums = call(
        functools.partial(forward_body, yn),
        [((experts, slots, quarter), BF16), ((XN, experts, 2 * units, slots), BF16)],
        flops, 4 << 20, at, at_y, *chunks, *weights,
    )
    sums = swap(sums, "x")
    hidden, grads = call(
        gate_body,
        [((experts, units, slots), BF16), ((XN, experts, 2 * units, slots), BF16)],
        20 * rows_w * slots, 1 << 20, sums, hidden_grad,
    )
    grads = swap(grads, "x")
    part, b0, b1, b2, b3 = call(
        backward_body,
        [((yn, experts, slots, LANES), BF16)] + [((rows_w, quarter), BF16)] * XN,
        2 * flops, 6 << 20, at, grads, *weights, rows,
    )
    parts = swap(part, "y")
    back = (b0,) + exchange_x(b1, b2, b3)
    (summed,) = call(
        sum_body, [((groups, experts, capacity, LANES), BF16)], 1 << 20, 2 << 20, parts
    )
    returned = swap(summed, "expert")
    (token_grad,) = call(
        fold_body, [(tokens.shape, BF16)], 1 << 22, 1 << 18, pick, returned.reshape(every, LANES)
    )
    (weight_grad,) = call(join_body, [((rows_w, width), BF16)], 0, 4 * rows_w * width, at, *back)
    return hidden, weight_grad.reshape(gate_up.shape), token_grad


def solution(mesh):
    n_expert, n_fsdp = mesh.devices.shape
    grid = Mesh(mesh.devices.reshape(n_expert, n_fsdp // XN, XN), ("expert", "y", "x"))
    fsdp = ("y", "x")
    placed = (
        P("expert", fsdp),
        P("expert", None),
        P("expert", None, fsdp, None),
        P("expert", fsdp, None),
    )
    return jax.shard_map(
        body,
        mesh=grid,
        in_specs=placed,
        out_specs=(P("expert", fsdp, None), P("expert", None, fsdp, None), P("expert", fsdp)),
        check_vma=False,
    )
```

profile of v0, /device:TPU:1, one launch (start us, length us, event | category | flops | bytes accessed | tf_op | source)
XLA Modules:
  0.0 162.5 jit_solution(9026954372374974505)
XLA Ops:
  0.6 1.8 %shard_map.67 = (bf16[512,128]{1,0:T(8,128)(2,1)}, bf16[512,32]{1,0:T(8,128)(2,1)}) custom-call(s32[8,32]{1,0:T(8,128)} %bitcast.16, bf16[32,128]{1,0:T(8,128)(2,1)} %tokens.1), custom_call_target="tpu_custom_call" | custom-call | flops 4194304 | bytes 262144 | tf_op jit(solution)/shard_map/pallas_call | solution.py:22
  2.5 20.4 %all-to-all-start = ((bf16[32,2,8,128]{3,2,1,0:T(8,128)(2,1)}), bf16[32,2,8,128]{3,2,1,0:T(8,128)(2,1)S(1)}, u32[]{:S(2)}, u32[]{:S(2)}) async-start(bf16[32,2,8,128]{3,2,1,0:T(8,128)(2,1)} %bitcast.15), calls=%async_computation | async-start | bytes 262144 | tf_op jit(solution)/shard_map/all_to_all | solution.py:42
  22.9 0.0 copy-start
  22.9 1.4 copy-done
  24.3 1.2 shard_map.68
  25.5 4.4 %collective-permute-start.8 = (bf16[192,1024]{1,0:T(8,128)(2,1)}, bf16[192,1024]{1,0:T(8,128)(2,1)S(1)}, u32[]{:S(2)}, u32[]{:S(2)}) collective-permute-start(bf16[192,1024]{1,0:T(8,128)(2,1)} %get-tuple-element.20), channel_id=1, source_target_pairs={{0,3},{1,0},{2,1},{3,2},{4,7},{5,4},{6,5},{7,6},{8,11},{9,8},{10,9... | collective-permute-start | bytes 1179656 | tf_op jit(solution)/shard_map/ppermute | solution.py:51
  29.8 2.4 %collective-permute-start.9 = (bf16[192,1024]{1,0:T(8,128)(2,1)S(1)}, bf16[192,1024]{1,0:T(8,128)(2,1)S(1)}, u32[]{:S(2)}, u32[]{:S(2)}) collective-permute-start(bf16[192,1024]{1,0:T(8,128)(2,1)S(1)} %get-tuple-element.21), channel_id=1, source_target_pairs={{0,2},{1,3},{2,0},{3,1},{4,6},{5,7},{6,4},{7,5},{8,10},{9,11},{10,... | collective-permute-start | bytes 1179656 | tf_op jit(solution)/shard_map/ppermute | solution.py:51
  32.3 2.5 %collective-permute-start.10 = (bf16[192,1024]{1,0:T(8,128)(2,1)S(1)}, bf16[192,1024]{1,0:T(8,128)(2,1)S(1)}, u32[]{:S(2)}, u32[]{:S(2)}) collective-permute-start(bf16[192,1024]{1,0:T(8,128)(2,1)S(1)} %get-tuple-element.22), channel_id=1, source_target_pairs={{0,1},{1,2},{2,3},{3,0},{4,5},{5,6},{6,7},{7,4},{8,9},{9,10},{10,1... | collective-permute-start | bytes 1179656 | tf_op jit(solution)/shard_map/ppermute | solution.py:51
  34.8 3.9 %all-to-all-done = bf16[32,2,8,128]{3,2,1,0:T(8,128)(2,1)S(1)} async-done(((bf16[32,2,8,128]{3,2,1,0:T(8,128)(2,1)}), bf16[32,2,8,128]{3,2,1,0:T(8,128)(2,1)S(1)}, u32[]{:S(2)}, u32[]{:S(2)}) %all-to-all-start) | async-done | bytes 131104 | tf_op jit(solution)/shard_map/all_to_all | solution.py:42
  38.7 3.2 %collective-permute-start.3 = (bf16[2,256,128]{2,1,0:T(8,128)(2,1)S(1)}, bf16[2,256,128]{2,1,0:T(8,128)(2,1)S(1)}, u32[]{:S(2)}, u32[]{:S(2)}) collective-permute-start(bf16[2,256,128]{2,1,0:T(8,128)(2,1)S(1)} %copy_bitcast_fusion.refs_0_), channel_id=1, source_target_pairs={{0,4},{4,8},{8,12},{12,16},{16,20},{20,24},{24,28},{28,0},{1,5},{5... | collective-permute-start | bytes 393224 | tf_op jit(solution)/shard_map/ppermute | solution.py:51
  41.9 3.8 %collective-permute-start = (bf16[2,256,128]{2,1,0:T(8,128)(2,1)S(1)}, bf16[2,256,128]{2,1,0:T(8,128)(2,1)S(1)}, u32[]{:S(2)}, u32[]{:S(2)}) collective-permute-start(bf16[2,256,128]{2,1,0:T(8,128)(2,1)S(1)} %copy_bitcast_fusion.refs_0_), channel_id=1, source_target_pairs={{0,28},{4,0},{8,4},{12,8},{16,12},{20,16},{24,20},{28,24},{1,29},{... | collective-permute-start | bytes 393224 | tf_op jit(solution)/shard_map/ppermute | solution.py:51
  45.8 0.7 collective-permute-done.3.refs_6_
  46.5 1.9 %collective-permute-start.4 = (bf16[2,256,128]{2,1,0:T(8,128)(2,1)S(1)}, bf16[2,256,128]{2,1,0:T(8,128)(2,1)S(1)}, u32[]{:S(2)}, u32[]{:S(2)}) collective-permute-start(bf16[2,256,128]{2,1,0:T(8,128)(2,1)S(1)} %collective-permute-done.3.refs_6_), channel_id=1, source_target_pairs={{0,4},{4,8},{8,12},{12,16},{16,20},{20,24},{24,28},{28,0},{1,5},{5... | collective-permute-start | bytes 393224 | tf_op jit(solution)/shard_map/ppermute | solution.py:51
  48.4 0.0 collective-permute-done.refs_1_
  48.4 4.6 %collective-permute-start.1 = (bf16[2,256,128]{2,1,0:T(8,128)(2,1)S(1)}, bf16[2,256,128]{2,1,0:T(8,128)(2,1)S(1)}, u32[]{:S(2)}, u32[]{:S(2)}) collective-permute-start(bf16[2,256,128]{2,1,0:T(8,128)(2,1)S(1)} %collective-permute-done.refs_1_), channel_id=1, source_target_pairs={{0,28},{4,0},{8,4},{12,8},{16,12},{20,16},{24,20},{28,24},{1,29},{... | collective-permute-start | bytes 393224 | tf_op jit(solution)/shard_map/ppermute | solution.py:51
  53.0 0.4 collective-permute-done.4.refs_5_
  53.4 1.9 %collective-permute-start.5 = (bf16[2,256,128]{2,1,0:T(8,128)(2,1)S(1)}, bf16[2,256,128]{2,1,0:T(8,128)(2,1)S(1)}, u32[]{:S(2)}, u32[]{:S(2)}) collective-permute-start(bf16[2,256,128]{2,1,0:T(8,128)(2,1)S(1)} %collective-permute-done.4.refs_5_), channel_id=1, source_target_pairs={{0,4},{4,8},{8,12},{12,16},{16,20},{20,24},{24,28},{28,0},{1,5},{5... | collective-permute-start | bytes 393224 | tf_op jit(solution)/shard_map/ppermute | solution.py:51
  55.3 0.0 collective-permute-done.1.refs_2_
  55.3 4.6 %collective-permute-start.2 = (bf16[2,256,128]{2,1,0:T(8,128)(2,1)S(1)}, bf16[2,256,128]{2,1,0:T(8,128)(2,1)S(1)}, u32[]{:S(2)}, u32[]{:S(2)}) collective-permute-start(bf16[2,256,128]{2,1,0:T(8,128)(2,1)S(1)} %collective-permute-done.1.refs_2_), channel_id=1, source_target_pairs={{0,28},{4,0},{8,4},{12,8},{16,12},{20,16},{24,20},{28,24},{1,29},{... | collective-permute-start | bytes 393224 | tf_op jit(solution)/shard_map/ppermute | solution.py:51
  59.9 0.0 collective-permute-done.8.refs_10_.refs_1_
  59.9 2.2 %collective-permute-start.6 = (bf16[1,256,128]{2,1,0:T(8,128)(2,1)S(1)}, bf16[1,256,128]{2,1,0:T(8,128)(2,1)S(1)}, u32[]{:S(2)}, u32[]{:S(2)}) collective-permute-start(bf16[1,256,128]{2,1,0:T(8,128)(2,1)S(1)} %slice.8), channel_id=1, source_target_pairs={{0,8},{4,12},{8,16},{12,20},{16,24},{20,28},{24,0},{28,4},{1,9},{5... | collective-permute-start | bytes 196616 | tf_op jit(solution)/shard_map/ppermute | solution.py:51
  62.1 0.0 collective-permute-done.9.refs_11_.refs_2_
  62.1 5.2 %collective-permute-start.7 = (bf16[1,256,128]{2,1,0:T(8,128)(2,1)S(1)}, bf16[1,256,128]{2,1,0:T(8,128)(2,1)S(1)}, u32[]{:S(2)}, u32[]{:S(2)}) collective-permute-start(bf16[1,256,128]{2,1,0:T(8,128)(2,1)S(1)} %slice.9), channel_id=1, source_target_pairs={{0,24},{4,28},{8,0},{12,4},{16,8},{20,12},{24,16},{28,20},{1,25},{... | collective-permute-start | bytes 196616 | tf_op jit(solution)/shard_map/ppermute | solution.py:51
  67.4 0.0 collective-permute-done.10.refs_12_.refs_3_
  67.4 0.0 collective-permute-done.6.refs_7_
  67.4 4.0 %collective-permute-done.7.refs_8_ = bf16[1,256,128]{2,1,0:T(8,128)(2,1)S(1)} collective-permute-done((bf16[1,256,128]{2,1,0:T(8,128)(2,1)S(1)}, bf16[1,256,128]{2,1,0:T(8,128)(2,1)S(1)}, u32[]{:S(2)}, u32[]{:S(2)}) %collective-permute-start.7) | collective-permute-done | bytes 65568 | tf_op jit(solution)/shard_map/ppermute | solution.py:51
  71.4 0.0 collective-permute-done.5.refs_4_
  71.4 0.0 collective-permute-done.2.refs_3_
  71.4 0.9 shard_map.69
  72.4 9.8 %all_to_all.25.sums = bf16[4,2,96,256]{3,2,1,0:T(8,128)(2,1)S(1)} all-to-all(bf16[4,2,96,256]{3,2,1,0:T(8,128)(2,1)S(1)} %get-tuple-element.23), channel_id=1, replica_groups=mesh['expert'=32,'y'=8,'x'=4] {'x'}, dimensions={0} | all-to-all | bytes 786432 | tf_op jit(solution)/shard_map/all_to_all | solution.py:42
  82.1 0.0 copy-done.2
  82.1 0.7 shard_map.70
  82.9 8.6 %all_to_all.26.grads = bf16[4,2,96,256]{3,2,1,0:T(8,128)(2,1)S(1)} all-to-all(bf16[4,2,96,256]{3,2,1,0:T(8,128)(2,1)S(1)} %get-tuple-element.25), channel_id=1, replica_groups=mesh['expert'=32,'y'=8,'x'=4] {'x'}, dimensions={0} | all-to-all | bytes 786432 | tf_op jit(solution)/shard_map/all_to_all | solution.py:42
  91.5 1.1 shard_map.71
  92.6 23.8 %all_to_all.27.parts = bf16[8,2,256,128]{3,2,1,0:T(8,128)(2,1)S(1)} all-to-all(bf16[8,2,256,128]{3,2,1,0:T(8,128)(2,1)S(1)} %get-tuple-element.32), channel_id=1, replica_groups=mesh['expert'=32,'y'=8,'x'=4] {'y'}, dimensions={0} | all-to-all | bytes 2097152 | tf_op jit(solution)/shard_map/all_to_all | solution.py:42
  116.4 0.8 shard_map.73
  117.2 17.3 %all-to-all-start.4 = ((bf16[32,2,8,128]{3,2,1,0:T(8,128)(2,1)}), bf16[32,2,8,128]{3,2,1,0:T(8,128)(2,1)S(1)}, u32[]{:S(2)}, u32[]{:S(2)}) async-start(bf16[32,2,8,128]{3,2,1,0:T(8,128)(2,1)} %shard_map.73), calls=%async_computation.4 | async-start | bytes 262144 | tf_op jit(solution)/shard_map/all_to_all | solution.py:42
  134.5 2.8 %collective-permute-start.11 = (bf16[192,1024]{1,0:T(8,128)(2,1)S(1)}, bf16[192,1024]{1,0:T(8,128)(2,1)S(1)}, u32[]{:S(2)}, u32[]{:S(2)}) collective-permute-start(bf16[192,1024]{1,0:T(8,128)(2,1)S(1)} %get-tuple-element.28), channel_id=1, source_target_pairs={{0,3},{1,0},{2,1},{3,2},{4,7},{5,4},{6,5},{7,6},{8,11},{9,8},{10,9... | collective-permute-start | bytes 1179656 | tf_op jit(solution)/shard_map/ppermute | solution.py:51
  137.3 3.1 %collective-permute-start.12 = (bf16[192,1024]{1,0:T(8,128)(2,1)S(1)}, bf16[192,1024]{1,0:T(8,128)(2,1)S(1)}, u32[]{:S(2)}, u32[]{:S(2)}) collective-permute-start(bf16[192,1024]{1,0:T(8,128)(2,1)S(1)} %get-tuple-element.29), channel_id=1, source_target_pairs={{0,2},{1,3},{2,0},{3,1},{4,6},{5,7},{6,4},{7,5},{8,10},{9,11},{10,... | collective-permute-start | bytes 1179656 | tf_op jit(solution)/shard_map/ppermute | solution.py:51
  140.4 1.9 %collective-permute-start.13 = (bf16[192,1024]{1,0:T(8,128)(2,1)S(1)}, bf16[192,1024]{1,0:T(8,128)(2,1)S(1)}, u32[]{:S(2)}, u32[]{:S(2)}) collective-permute-start(bf16[192,1024]{1,0:T(8,128)(2,1)S(1)} %get-tuple-element.30), channel_id=1, source_target_pairs={{0,1},{1,2},{2,3},{3,0},{4,5},{5,6},{6,7},{7,4},{8,9},{9,10},{10,1... | collective-permute-start | bytes 1179656 | tf_op jit(solution)/shard_map/ppermute | solution.py:51
  142.3 4.5 %collective-permute-done.11.refs_1_ = bf16[192,1024]{1,0:T(8,128)(2,1)S(1)} collective-permute-done((bf16[192,1024]{1,0:T(8,128)(2,1)S(1)}, bf16[192,1024]{1,0:T(8,128)(2,1)S(1)}, u32[]{:S(2)}, u32[]{:S(2)}) %collective-permute-start.11) | collective-permute-done | bytes 393248 | tf_op jit(solution)/shard_map/ppermute | solution.py:51
  146.8 4.1 %collective-permute-done.12.refs_2_ = bf16[192,1024]{1,0:T(8,128)(2,1)S(1)} collective-permute-done((bf16[192,1024]{1,0:T(8,128)(2,1)S(1)}, bf16[192,1024]{1,0:T(8,128)(2,1)S(1)}, u32[]{:S(2)}, u32[]{:S(2)}) %collective-permute-start.12) | collective-permute-done | bytes 393248 | tf_op jit(solution)/shard_map/ppermute | solution.py:51
  150.9 9.3 %collective-permute-done.13.refs_3_ = bf16[192,1024]{1,0:T(8,128)(2,1)S(1)} collective-permute-done((bf16[192,1024]{1,0:T(8,128)(2,1)S(1)}, bf16[192,1024]{1,0:T(8,128)(2,1)S(1)}, u32[]{:S(2)}, u32[]{:S(2)}) %collective-permute-start.13) | collective-permute-done | bytes 393248 | tf_op jit(solution)/shard_map/ppermute | solution.py:51
  160.2 0.0 copy-start.1
  160.2 1.5 shard_map.72
  161.7 0.0 all-to-all-done.4
  161.7 0.0 copy-done.1
  161.7 0.8 shard_map.74
  (4 shorter events, 0.0 us)
Async XLA Ops:
  2.5 36.3 %all-to-all-start = ((bf16[32,2,8,128]{3,2,1,0:T(8,128)(2,1)}), bf16[32,2,8,128]{3,2,1,0:T(8,128)(2,1)S(1)}, u32[]{:S(2)}, u32[]{:S(2)}) async-start(bf16[32,2,8,128]{3,2,1,0:T(8,128)(2,1)} %bitcast.15), calls=%async_computation | async-start | bytes 262144 | tf_op jit(solution)/shard_map/all_to_all | solution.py:42
  22.9 1.4 copy-start
  25.5 34.5 %collective-permute-start.8 = (bf16[192,1024]{1,0:T(8,128)(2,1)}, bf16[192,1024]{1,0:T(8,128)(2,1)S(1)}, u32[]{:S(2)}, u32[]{:S(2)}) collective-permute-start(bf16[192,1024]{1,0:T(8,128)(2,1)} %get-tuple-element.20), channel_id=1, source_target_pairs={{0,3},{1,0},{2,1},{3,2},{4,7},{5,4},{6,5},{7,6},{8,11},{9,8},{10,9... | collective-permute-start | bytes 1179656 | tf_op jit(solution)/shard_map/ppermute | solution.py:51
  29.8 32.3 %collective-permute-start.9 = (bf16[192,1024]{1,0:T(8,128)(2,1)S(1)}, bf16[192,1024]{1,0:T(8,128)(2,1)S(1)}, u32[]{:S(2)}, u32[]{:S(2)}) collective-permute-start(bf16[192,1024]{1,0:T(8,128)(2,1)S(1)} %get-tuple-element.21), channel_id=1, source_target_pairs={{0,2},{1,3},{2,0},{3,1},{4,6},{5,7},{6,4},{7,5},{8,10},{9,11},{10,... | collective-permute-start | bytes 1179656 | tf_op jit(solution)/shard_map/ppermute | solution.py:51
  32.3 35.1 %collective-permute-start.10 = (bf16[192,1024]{1,0:T(8,128)(2,1)S(1)}, bf16[192,1024]{1,0:T(8,128)(2,1)S(1)}, u32[]{:S(2)}, u32[]{:S(2)}) collective-permute-start(bf16[192,1024]{1,0:T(8,128)(2,1)S(1)} %get-tuple-element.22), channel_id=1, source_target_pairs={{0,1},{1,2},{2,3},{3,0},{4,5},{5,6},{6,7},{7,4},{8,9},{9,10},{10,1... | collective-permute-start | bytes 1179656 | tf_op jit(solution)/shard_map/ppermute | solution.py:51
  38.7 7.7 %collective-permute-start.3 = (bf16[2,256,128]{2,1,0:T(8,128)(2,1)S(1)}, bf16[2,256,128]{2,1,0:T(8,128)(2,1)S(1)}, u32[]{:S(2)}, u32[]{:S(2)}) collective-permute-start(bf16[2,256,128]{2,1,0:T(8,128)(2,1)S(1)} %copy_bitcast_fusion.refs_0_), channel_id=1, source_target_pairs={{0,4},{4,8},{8,12},{12,16},{16,20},{20,24},{24,28},{28,0},{1,5},{5... | collective-permute-start | bytes 393224 | tf_op jit(solution)/shard_map/ppermute | solution.py:51
  41.9 6.4 %collective-permute-start = (bf16[2,256,128]{2,1,0:T(8,128)(2,1)S(1)}, bf16[2,256,128]{2,1,0:T(8,128)(2,1)S(1)}, u32[]{:S(2)}, u32[]{:S(2)}) collective-permute-start(bf16[2,256,128]{2,1,0:T(8,128)(2,1)S(1)} %copy_bitcast_fusion.refs_0_), channel_id=1, source_target_pairs={{0,28},{4,0},{8,4},{12,8},{16,12},{20,16},{24,20},{28,24},{1,29},{... | collective-permute-start | bytes 393224 | tf_op jit(solution)/shard_map/ppermute | solution.py:51
  46.5 6.9 %collective-permute-start.4 = (bf16[2,256,128]{2,1,0:T(8,128)(2,1)S(1)}, bf16[2,256,128]{2,1,0:T(8,128)(2,1)S(1)}, u32[]{:S(2)}, u32[]{:S(2)}) collective-permute-start(bf16[2,256,128]{2,1,0:T(8,128)(2,1)S(1)} %collective-permute-done.3.refs_6_), channel_id=1, source_target_pairs={{0,4},{4,8},{8,12},{12,16},{16,20},{20,24},{24,28},{28,0},{1,5},{5... | collective-permute-start | bytes 393224 | tf_op jit(solution)/shard_map/ppermute | solution.py:51
  48.4 6.9 %collective-permute-start.1 = (bf16[2,256,128]{2,1,0:T(8,128)(2,1)S(1)}, bf16[2,256,128]{2,1,0:T(8,128)(2,1)S(1)}, u32[]{:S(2)}, u32[]{:S(2)}) collective-permute-start(bf16[2,256,128]{2,1,0:T(8,128)(2,1)S(1)} %collective-permute-done.refs_1_), channel_id=1, source_target_pairs={{0,28},{4,0},{8,4},{12,8},{16,12},{20,16},{24,20},{28,24},{1,29},{... | collective-permute-start | bytes 393224 | tf_op jit(solution)/shard_map/ppermute | solution.py:51
  53.4 18.0 %collective-permute-start.5 = (bf16[2,256,128]{2,1,0:T(8,128)(2,1)S(1)}, bf16[2,256,128]{2,1,0:T(8,128)(2,1)S(1)}, u32[]{:S(2)}, u32[]{:S(2)}) collective-permute-start(bf16[2,256,128]{2,1,0:T(8,128)(2,1)S(1)} %collective-permute-done.4.refs_5_), channel_id=1, source_target_pairs={{0,4},{4,8},{8,12},{12,16},{16,20},{20,24},{24,28},{28,0},{1,5},{5... | collective-permute-start | bytes 393224 | tf_op jit(solution)/shard_map/ppermute | solution.py:51
  55.3 16.1 %collective-permute-start.2 = (bf16[2,256,128]{2,1,0:T(8,128)(2,1)S(1)}, bf16[2,256,128]{2,1,0:T(8,128)(2,1)S(1)}, u32[]{:S(2)}, u32[]{:S(2)}) collective-permute-start(bf16[2,256,128]{2,1,0:T(8,128)(2,1)S(1)} %collective-permute-done.1.refs_2_), channel_id=1, source_target_pairs={{0,28},{4,0},{8,4},{12,8},{16,12},{20,16},{24,20},{28,24},{1,29},{... | collective-permute-start | bytes 393224 | tf_op jit(solution)/shard_map/ppermute | solution.py:51
  59.9 7.4 %collective-permute-start.6 = (bf16[1,256,128]{2,1,0:T(8,128)(2,1)S(1)}, bf16[1,256,128]{2,1,0:T(8,128)(2,1)S(1)}, u32[]{:S(2)}, u32[]{:S(2)}) collective-permute-start(bf16[1,256,128]{2,1,0:T(8,128)(2,1)S(1)} %slice.8), channel_id=1, source_target_pairs={{0,8},{4,12},{8,16},{12,20},{16,24},{20,28},{24,0},{28,4},{1,9},{5... | collective-permute-start | bytes 196616 | tf_op jit(solution)/shard_map/ppermute | solution.py:51
  62.1 9.3 %collective-permute-start.7 = (bf16[1,256,128]{2,1,0:T(8,128)(2,1)S(1)}, bf16[1,256,128]{2,1,0:T(8,128)(2,1)S(1)}, u32[]{:S(2)}, u32[]{:S(2)}) collective-permute-start(bf16[1,256,128]{2,1,0:T(8,128)(2,1)S(1)} %slice.9), channel_id=1, source_target_pairs={{0,24},{4,28},{8,0},{12,4},{16,8},{20,12},{24,16},{28,20},{1,25},{... | collective-permute-start | bytes 196616 | tf_op jit(solution)/shard_map/ppermute | solution.py:51
  71.4 10.7 %copy-start.2 = (bf16[2,48,256]{2,1,0:T(8,128)(2,1)S(1)}, bf16[2,48,256]{2,1,0:T(8,128)(2,1)}, u32[]{:S(2)}) copy-start(bf16[2,48,256]{2,1,0:T(8,128)(2,1)} %hg.1) | copy-start | bytes 147460
  117.2 44.5 %all-to-all-start.4 = ((bf16[32,2,8,128]{3,2,1,0:T(8,128)(2,1)}), bf16[32,2,8,128]{3,2,1,0:T(8,128)(2,1)S(1)}, u32[]{:S(2)}, u32[]{:S(2)}) async-start(bf16[32,2,8,128]{3,2,1,0:T(8,128)(2,1)} %shard_map.73), calls=%async_computation.4 | async-start | bytes 262144 | tf_op jit(solution)/shard_map/all_to_all | solution.py:42
  134.5 12.3 %collective-permute-start.11 = (bf16[192,1024]{1,0:T(8,128)(2,1)S(1)}, bf16[192,1024]{1,0:T(8,128)(2,1)S(1)}, u32[]{:S(2)}, u32[]{:S(2)}) collective-permute-start(bf16[192,1024]{1,0:T(8,128)(2,1)S(1)} %get-tuple-element.28), channel_id=1, source_target_pairs={{0,3},{1,0},{2,1},{3,2},{4,7},{5,4},{6,5},{7,6},{8,11},{9,8},{10,9... | collective-permute-start | bytes 1179656 | tf_op jit(solution)/shard_map/ppermute | solution.py:51
  137.3 13.6 %collective-permute-start.12 = (bf16[192,1024]{1,0:T(8,128)(2,1)S(1)}, bf16[192,1024]{1,0:T(8,128)(2,1)S(1)}, u32[]{:S(2)}, u32[]{:S(2)}) collective-permute-start(bf16[192,1024]{1,0:T(8,128)(2,1)S(1)} %get-tuple-element.29), channel_id=1, source_target_pairs={{0,2},{1,3},{2,0},{3,1},{4,6},{5,7},{6,4},{7,5},{8,10},{9,11},{10,... | collective-permute-start | bytes 1179656 | tf_op jit(solution)/shard_map/ppermute | solution.py:51
  140.4 19.8 %collective-permute-start.13 = (bf16[192,1024]{1,0:T(8,128)(2,1)S(1)}, bf16[192,1024]{1,0:T(8,128)(2,1)S(1)}, u32[]{:S(2)}, u32[]{:S(2)}) collective-permute-start(bf16[192,1024]{1,0:T(8,128)(2,1)S(1)} %get-tuple-element.30), channel_id=1, source_target_pairs={{0,1},{1,2},{2,3},{3,0},{4,5},{5,6},{6,7},{7,4},{8,9},{9,10},{10,1... | collective-permute-start | bytes 1179656 | tf_op jit(solution)/shard_map/ppermute | solution.py:51
  160.2 1.5 copy-start.1
where the time goes:
time: 163 us; the launch traced here: 162 us
  starting transfers between devices  82.2 us (50%)
  blocking collectives  42.2 us (26%)
  waiting for transfers between devices  26.9 us (17%)
  Pallas kernels  8.87 us (5%)
    ppermute x14, starting transfers between devices, shift(): return lax.ppermute(v, axis, [(i, (i + k) % n) for i in range(n)])  44.5 us
    all_to_all x3, blocking collectives, swap(): return lax.all_to_all(v, axis, split_axis=0, concat_axis=0, tiled=True)  42.2 us
    all_to_all x2, starting transfers between devices, swap(): return lax.all_to_all(v, axis, split_axis=0, concat_axis=0, tiled=True)  37.7 us
    ppermute x14, waiting for transfers between devices, shift(): return lax.ppermute(v, axis, [(i, (i + k) % n) for i in range(n)])  23 us
    pallas_call x8, Pallas kernels, call(): pl.pallas_call(body, out_shape=[jax.ShapeDtypeStruct(s, d) for s, d in ou...  8.87 us
    all_to_all x2, waiting for transfers between devices, swap(): return lax.all_to_all(v, axis, split_axis=0, concat_axis=0, tiled=True)  3.93 us
  transfers between devices with their start and end apart: 16, of which 7 were waited for; matrix products, arithmetic and copies ran while one was open for 0% of the time, Pallas kernels for 2%

commit v1 on v0

--- a/solution.py
+++ b/solution.py
@@ -54,16 +54,12 @@
 def gather_y(own):
     n = lax.axis_size("y")
     half = n // 2
-    near = {0: own}
-    up, down = own, own
-    middle = own.shape[0] // 2
-    for k in range(1, half):
-        if k == half - 1:
-            last = [(up[:middle], 2), (down[middle:], -2)]
+    up, down = shift(own, "y", 1), shift(own, "y", -1)
+    got = {0: own, half: shift(own, "y", half), n - 1: up, 1: down}
+    for k in range(2, half):
         up, down = shift(up, "y", 1), shift(down, "y", -1)
-        near[n - k], near[k] = up, down
-    last = [shift(v, "y", k) for v, k in last]
-    return [near[k] for k in range(n) if k != half] + last
+        got[n - k], got[k] = up, down
+    return [got[k] for k in range(n)]
 
 
 def exchange_x(v1, v2, v3):
@@ -88,17 +84,14 @@
 
 
 def forward_body(yn, at, at_y, *refs):
-    chunks, last, refs = refs[: yn - 1], refs[yn - 1 : yn + 1], refs[yn + 1 :]
+    chunks, refs = refs[:yn], refs[yn:]
     weights, rows, sums = refs[:XN], refs[XN], refs[XN + 1]
-    experts, half = rows.shape[0], yn // 2
+    experts = rows.shape[0]
     units = weights[0].shape[0] // experts
     for e in range(experts):
         for k in range(yn):
             where = lane_block(lax.rem(at_y[0] + k, yn))
-            if k == half:
-                rows[e, :, where] = last[2 * e // experts][e % (experts // 2)]
-            else:
-                rows[e, :, where] = chunks[k if k < half else k - 1][e]
+            rows[e, :, where] = chunks[k][e]
         left = jnp.concatenate([w[e * units : (e + 1) * units] for w in weights], axis=0)
         total = dot(left, rows[e], 1, 1).astype(BF16)
         for j in range(XN):

time: 163 us -> 162 us (level)
    all_to_all x2, waiting for transfers between devices: 3.93 us -> 7.18 us  [swap(): return lax.all_to_all(v, axis, split_axis=0, concat_axis=0, tiled=True)]
    ppermute x14 -> x13, waiting for transfers between devices: 23 us -> 20 us  [shift(): return lax.ppermute(v, axis, [(i, (i + k) % n) for i in range(n)])]
    ppermute x14 -> x13, starting transfers between devices: 44.5 us -> 45.1 us  [shift(): return lax.ppermute(v, axis, [(i, (i + k) % n) for i in range(n)])]
  transfers between devices with their start and end apart: 16 -> 15, of which waited for: 7 -> 7; matrix products, arithmetic and copies ran while one was open for 0% -> 0% of each run, Pallas kernels for 2% -> 1%
where the time goes in v1:
time: 162 us; the launch traced here: 161 us
  starting transfers between devices  81.3 us (50%)
  blocking collectives  42.3 us (26%)
  waiting for transfers between devices  27.2 us (17%)
  Pallas kernels  8.11 us (5%)
    ppermute x13, starting transfers between devices, shift(): return lax.ppermute(v, axis, [(i, (i + k) % n) for i in range(n)])  45.1 us
    all_to_all x3, blocking collectives, swap(): return lax.all_to_all(v, axis, split_axis=0, concat_axis=0, tiled=True)  42.3 us
    all_to_all x2, starting transfers between devices, swap(): return lax.all_to_all(v, axis, split_axis=0, concat_axis=0, tiled=True)  36.2 us
    ppermute x13, waiting for transfers between devices, shift(): return lax.ppermute(v, axis, [(i, (i + k) % n) for i in range(n)])  20 us
    pallas_call x8, Pallas kernels, call(): pl.pallas_call(body, out_shape=[jax.ShapeDtypeStruct(s, d) for s, d in ou...  8.11 us
    all_to_all x2, waiting for transfers between devices, swap(): return lax.all_to_all(v, axis, split_axis=0, concat_axis=0, tiled=True)  7.18 us
  transfers between devices with their start and end apart: 15, of which 7 were waited for; matrix products, arithmetic and copies ran while one was open for 0% of the time, Pallas kernels for 1%

profile of v1, /device:TPU:1, one launch (start us, length us, event | category | flops | bytes accessed | tf_op | source)
XLA Modules:
  0.0 161.2 jit_solution(7884451679140315828)
XLA Ops:
  0.6 1.8 %shard_map.67 = (bf16[512,128]{1,0:T(8,128)(2,1)}, bf16[512,32]{1,0:T(8,128)(2,1)}) custom-call(s32[8,32]{1,0:T(8,128)} %bitcast.16, bf16[32,128]{1,0:T(8,128)(2,1)} %tokens.1), custom_call_target="tpu_custom_call" | custom-call | flops 4194304 | bytes 262144 | tf_op jit(solution)/shard_map/pallas_call | solution.py:22
  2.5 20.4 %all-to-all-start = ((bf16[32,2,8,128]{3,2,1,0:T(8,128)(2,1)}), bf16[32,2,8,128]{3,2,1,0:T(8,128)(2,1)S(1)}, u32[]{:S(2)}, u32[]{:S(2)}) async-start(bf16[32,2,8,128]{3,2,1,0:T(8,128)(2,1)} %bitcast.15), calls=%async_computation | async-start | bytes 262144 | tf_op jit(solution)/shard_map/all_to_all | solution.py:42
  22.9 0.0 copy-start
  22.9 1.4 copy-done
  24.3 0.4 shard_map.68
  24.7 4.4 %collective-permute-start.7 = (bf16[192,1024]{1,0:T(8,128)(2,1)S(1)}, bf16[192,1024]{1,0:T(8,128)(2,1)S(1)}, u32[]{:S(2)}, u32[]{:S(2)}) collective-permute-start(bf16[192,1024]{1,0:T(8,128)(2,1)S(1)} %get-tuple-element.20), channel_id=1, source_target_pairs={{0,3},{1,0},{2,1},{3,2},{4,7},{5,4},{6,5},{7,6},{8,11},{9,8},{10,9... | collective-permute-start | bytes 1179656 | tf_op jit(solution)/shard_map/ppermute | solution.py:51
  29.1 2.4 %collective-permute-start.8 = (bf16[192,1024]{1,0:T(8,128)(2,1)S(1)}, bf16[192,1024]{1,0:T(8,128)(2,1)S(1)}, u32[]{:S(2)}, u32[]{:S(2)}) collective-permute-start(bf16[192,1024]{1,0:T(8,128)(2,1)S(1)} %get-tuple-element.21), channel_id=1, source_target_pairs={{0,2},{1,3},{2,0},{3,1},{4,6},{5,7},{6,4},{7,5},{8,10},{9,11},{10,... | collective-permute-start | bytes 1179656 | tf_op jit(solution)/shard_map/ppermute | solution.py:51
  31.5 7.2 %all-to-all-done = bf16[32,2,8,128]{3,2,1,0:T(8,128)(2,1)S(1)} async-done(((bf16[32,2,8,128]{3,2,1,0:T(8,128)(2,1)}), bf16[32,2,8,128]{3,2,1,0:T(8,128)(2,1)S(1)}, u32[]{:S(2)}, u32[]{:S(2)}) %all-to-all-start) | async-done | bytes 131104 | tf_op jit(solution)/shard_map/all_to_all | solution.py:42
  38.7 3.2 %collective-permute-start.4 = (bf16[2,256,128]{2,1,0:T(8,128)(2,1)S(1)}, bf16[2,256,128]{2,1,0:T(8,128)(2,1)S(1)}, u32[]{:S(2)}, u32[]{:S(2)}) collective-permute-start(bf16[2,256,128]{2,1,0:T(8,128)(2,1)S(1)} %copy_bitcast_fusion.refs_0_), channel_id=1, source_target_pairs={{0,4},{4,8},{8,12},{12,16},{16,20},{20,24},{24,28},{28,0},{1,5},{5... | collective-permute-start | bytes 393224 | tf_op jit(solution)/shard_map/ppermute | solution.py:51
  41.9 3.1 %collective-permute-start.9 = (bf16[192,1024]{1,0:T(8,128)(2,1)S(1)}, bf16[192,1024]{1,0:T(8,128)(2,1)S(1)}, u32[]{:S(2)}, u32[]{:S(2)}) collective-permute-start(bf16[192,1024]{1,0:T(8,128)(2,1)S(1)} %get-tuple-element.22), channel_id=1, source_target_pairs={{0,1},{1,2},{2,3},{3,0},{4,5},{5,6},{6,7},{7,4},{8,9},{9,10},{10,1... | collective-permute-start | bytes 1179656 | tf_op jit(solution)/shard_map/ppermute | solution.py:51
  45.1 3.8 %collective-permute-start = (bf16[2,256,128]{2,1,0:T(8,128)(2,1)S(1)}, bf16[2,256,128]{2,1,0:T(8,128)(2,1)S(1)}, u32[]{:S(2)}, u32[]{:S(2)}) collective-permute-start(bf16[2,256,128]{2,1,0:T(8,128)(2,1)S(1)} %copy_bitcast_fusion.refs_0_), channel_id=1, source_target_pairs={{0,28},{4,0},{8,4},{12,8},{16,12},{20,16},{24,20},{28,24},{1,29},{... | collective-permute-start | bytes 393224 | tf_op jit(solution)/shard_map/ppermute | solution.py:51
  48.9 0.0 collective-permute-done.4.refs_7_
  48.9 1.9 %collective-permute-start.5 = (bf16[2,256,128]{2,1,0:T(8,128)(2,1)S(1)}, bf16[2,256,128]{2,1,0:T(8,128)(2,1)S(1)}, u32[]{:S(2)}, u32[]{:S(2)}) collective-permute-start(bf16[2,256,128]{2,1,0:T(8,128)(2,1)S(1)} %collective-permute-done.4.refs_7_), channel_id=1, source_target_pairs={{0,4},{4,8},{8,12},{12,16},{16,20},{20,24},{24,28},{28,0},{1,5},{5... | collective-permute-start | bytes 393224 | tf_op jit(solution)/shard_map/ppermute | solution.py:51
  50.8 0.2 collective-permute-done.refs_1_
  51.1 5.0 %collective-permute-start.1 = (bf16[2,256,128]{2,1,0:T(8,128)(2,1)S(1)}, bf16[2,256,128]{2,1,0:T(8,128)(2,1)S(1)}, u32[]{:S(2)}, u32[]{:S(2)}) collective-permute-start(bf16[2,256,128]{2,1,0:T(8,128)(2,1)S(1)} %collective-permute-done.refs_1_), channel_id=1, source_target_pairs={{0,28},{4,0},{8,4},{12,8},{16,12},{20,16},{24,20},{28,24},{1,29},{... | collective-permute-start | bytes 393224 | tf_op jit(solution)/shard_map/ppermute | solution.py:51
  56.1 0.0 collective-permute-done.7.refs_9_.refs_1_
  56.1 6.9 %collective-permute-start.3 = (bf16[2,256,128]{2,1,0:T(8,128)(2,1)S(1)}, bf16[2,256,128]{2,1,0:T(8,128)(2,1)S(1)}, u32[]{:S(2)}, u32[]{:S(2)}) collective-permute-start(bf16[2,256,128]{2,1,0:T(8,128)(2,1)S(1)} %copy_bitcast_fusion.refs_0_), channel_id=1, source_target_pairs={{0,16},{4,20},{8,24},{12,28},{16,0},{20,4},{24,8},{28,12},{1,17},{... | collective-permute-start | bytes 393224 | tf_op jit(solution)/shard_map/ppermute | solution.py:51
  63.1 0.0 collective-permute-done.5.refs_6_
  63.1 1.9 %collective-permute-start.6 = (bf16[2,256,128]{2,1,0:T(8,128)(2,1)S(1)}, bf16[2,256,128]{2,1,0:T(8,128)(2,1)S(1)}, u32[]{:S(2)}, u32[]{:S(2)}) collective-permute-start(bf16[2,256,128]{2,1,0:T(8,128)(2,1)S(1)} %collective-permute-done.5.refs_6_), channel_id=1, source_target_pairs={{0,4},{4,8},{8,12},{12,16},{16,20},{20,24},{24,28},{28,0},{1,5},{5... | collective-permute-start | bytes 393224 | tf_op jit(solution)/shard_map/ppermute | solution.py:51
  65.0 0.0 collective-permute-done.1.refs_2_
  65.0 4.6 %collective-permute-start.2 = (bf16[2,256,128]{2,1,0:T(8,128)(2,1)S(1)}, bf16[2,256,128]{2,1,0:T(8,128)(2,1)S(1)}, u32[]{:S(2)}, u32[]{:S(2)}) collective-permute-start(bf16[2,256,128]{2,1,0:T(8,128)(2,1)S(1)} %collective-permute-done.1.refs_2_), channel_id=1, source_target_pairs={{0,28},{4,0},{8,4},{12,8},{16,12},{20,16},{24,20},{28,24},{1,29},{... | collective-permute-start | bytes 393224 | tf_op jit(solution)/shard_map/ppermute | solution.py:51
  69.6 0.0 collective-permute-done.8.refs_10_.refs_2_
  69.6 0.0 collective-permute-done.9.refs_11_.refs_3_
  69.6 0.0 collective-permute-done.3.refs_4_
  69.6 1.4 collective-permute-done.6.refs_5_
  71.0 0.5 collective-permute-done.2.refs_3_
  71.5 0.0 copy-start.2
  71.5 0.9 shard_map.69
  72.4 9.5 %all_to_all.25.sums = bf16[4,2,96,256]{3,2,1,0:T(8,128)(2,1)S(1)} all-to-all(bf16[4,2,96,256]{3,2,1,0:T(8,128)(2,1)S(1)} %get-tuple-element.23), channel_id=1, replica_groups=mesh['expert'=32,'y'=8,'x'=4] {'x'}, dimensions={0} | all-to-all | bytes 786432 | tf_op jit(solution)/shard_map/all_to_all | solution.py:42
  81.9 0.0 copy-done.2
  81.9 0.7 shard_map.70
  82.6 8.6 %all_to_all.26.grads = bf16[4,2,96,256]{3,2,1,0:T(8,128)(2,1)S(1)} all-to-all(bf16[4,2,96,256]{3,2,1,0:T(8,128)(2,1)S(1)} %get-tuple-element.25), channel_id=1, replica_groups=mesh['expert'=32,'y'=8,'x'=4] {'x'}, dimensions={0} | all-to-all | bytes 786432 | tf_op jit(solution)/shard_map/all_to_all | solution.py:42
  91.2 1.1 shard_map.71
  92.4 24.2 %all_to_all.27.parts = bf16[8,2,256,128]{3,2,1,0:T(8,128)(2,1)S(1)} all-to-all(bf16[8,2,256,128]{3,2,1,0:T(8,128)(2,1)S(1)} %get-tuple-element.32), channel_id=1, replica_groups=mesh['expert'=32,'y'=8,'x'=4] {'y'}, dimensions={0} | all-to-all | bytes 2097152 | tf_op jit(solution)/shard_map/all_to_all | solution.py:42
  116.6 0.8 shard_map.73
  117.4 15.8 %all-to-all-start.4 = ((bf16[32,2,8,128]{3,2,1,0:T(8,128)(2,1)}), bf16[32,2,8,128]{3,2,1,0:T(8,128)(2,1)S(1)}, u32[]{:S(2)}, u32[]{:S(2)}) async-start(bf16[32,2,8,128]{3,2,1,0:T(8,128)(2,1)} %shard_map.73), calls=%async_computation.4 | async-start | bytes 262144 | tf_op jit(solution)/shard_map/all_to_all | solution.py:42
  133.2 2.8 %collective-permute-start.10 = (bf16[192,1024]{1,0:T(8,128)(2,1)S(1)}, bf16[192,1024]{1,0:T(8,128)(2,1)S(1)}, u32[]{:S(2)}, u32[]{:S(2)}) collective-permute-start(bf16[192,1024]{1,0:T(8,128)(2,1)S(1)} %get-tuple-element.28), channel_id=1, source_target_pairs={{0,3},{1,0},{2,1},{3,2},{4,7},{5,4},{6,5},{7,6},{8,11},{9,8},{10,9... | collective-permute-start | bytes 1179656 | tf_op jit(solution)/shard_map/ppermute | solution.py:51
  136.0 3.1 %collective-permute-start.11 = (bf16[192,1024]{1,0:T(8,128)(2,1)S(1)}, bf16[192,1024]{1,0:T(8,128)(2,1)S(1)}, u32[]{:S(2)}, u32[]{:S(2)}) collective-permute-start(bf16[192,1024]{1,0:T(8,128)(2,1)S(1)} %get-tuple-element.29), channel_id=1, source_target_pairs={{0,2},{1,3},{2,0},{3,1},{4,6},{5,7},{6,4},{7,5},{8,10},{9,11},{10,... | collective-permute-start | bytes 1179656 | tf_op jit(solution)/shard_map/ppermute | solution.py:51
  139.1 1.9 %collective-permute-start.12 = (bf16[192,1024]{1,0:T(8,128)(2,1)S(1)}, bf16[192,1024]{1,0:T(8,128)(2,1)S(1)}, u32[]{:S(2)}, u32[]{:S(2)}) collective-permute-start(bf16[192,1024]{1,0:T(8,128)(2,1)S(1)} %get-tuple-element.30), channel_id=1, source_target_pairs={{0,1},{1,2},{2,3},{3,0},{4,5},{5,6},{6,7},{7,4},{8,9},{9,10},{10,1... | collective-permute-start | bytes 1179656 | tf_op jit(solution)/shard_map/ppermute | solution.py:51
  141.0 4.5 %collective-permute-done.10.refs_1_ = bf16[192,1024]{1,0:T(8,128)(2,1)S(1)} collective-permute-done((bf16[192,1024]{1,0:T(8,128)(2,1)S(1)}, bf16[192,1024]{1,0:T(8,128)(2,1)S(1)}, u32[]{:S(2)}, u32[]{:S(2)}) %collective-permute-start.10) | collective-permute-done | bytes 393248 | tf_op jit(solution)/shard_map/ppermute | solution.py:51
  145.5 4.1 %collective-permute-done.11.refs_2_ = bf16[192,1024]{1,0:T(8,128)(2,1)S(1)} collective-permute-done((bf16[192,1024]{1,0:T(8,128)(2,1)S(1)}, bf16[192,1024]{1,0:T(8,128)(2,1)S(1)}, u32[]{:S(2)}, u32[]{:S(2)}) %collective-permute-start.11) | collective-permute-done | bytes 393248 | tf_op jit(solution)/shard_map/ppermute | solution.py:51
  149.6 9.3 %collective-permute-done.12.refs_3_ = bf16[192,1024]{1,0:T(8,128)(2,1)S(1)} collective-permute-done((bf16[192,1024]{1,0:T(8,128)(2,1)S(1)}, bf16[192,1024]{1,0:T(8,128)(2,1)S(1)}, u32[]{:S(2)}, u32[]{:S(2)}) %collective-permute-start.12) | collective-permute-done | bytes 393248 | tf_op jit(solution)/shard_map/ppermute | solution.py:51
  158.9 0.0 copy-start.1
  158.9 1.5 shard_map.72
  160.4 0.0 all-to-all-done.4
  160.4 0.0 copy-done.1
  160.4 0.8 shard_map.74
  (1 shorter events, 0.0 us)
Async XLA Ops:
  2.5 36.3 %all-to-all-start = ((bf16[32,2,8,128]{3,2,1,0:T(8,128)(2,1)}), bf16[32,2,8,128]{3,2,1,0:T(8,128)(2,1)S(1)}, u32[]{:S(2)}, u32[]{:S(2)}) async-start(bf16[32,2,8,128]{3,2,1,0:T(8,128)(2,1)} %bitcast.15), calls=%async_computation | async-start | bytes 262144 | tf_op jit(solution)/shard_map/all_to_all | solution.py:42
  22.9 1.4 copy-start
  24.7 31.4 %collective-permute-start.7 = (bf16[192,1024]{1,0:T(8,128)(2,1)S(1)}, bf16[192,1024]{1,0:T(8,128)(2,1)S(1)}, u32[]{:S(2)}, u32[]{:S(2)}) collective-permute-start(bf16[192,1024]{1,0:T(8,128)(2,1)S(1)} %get-tuple-element.20), channel_id=1, source_target_pairs={{0,3},{1,0},{2,1},{3,2},{4,7},{5,4},{6,5},{7,6},{8,11},{9,8},{10,9... | collective-permute-start | bytes 1179656 | tf_op jit(solution)/shard_map/ppermute | solution.py:51
  29.1 40.5 %collective-permute-start.8 = (bf16[192,1024]{1,0:T(8,128)(2,1)S(1)}, bf16[192,1024]{1,0:T(8,128)(2,1)S(1)}, u32[]{:S(2)}, u32[]{:S(2)}) collective-permute-start(bf16[192,1024]{1,0:T(8,128)(2,1)S(1)} %get-tuple-element.21), channel_id=1, source_target_pairs={{0,2},{1,3},{2,0},{3,1},{4,6},{5,7},{6,4},{7,5},{8,10},{9,11},{10,... | collective-permute-start | bytes 1179656 | tf_op jit(solution)/shard_map/ppermute | solution.py:51
  38.7 10.2 %collective-permute-start.4 = (bf16[2,256,128]{2,1,0:T(8,128)(2,1)S(1)}, bf16[2,256,128]{2,1,0:T(8,128)(2,1)S(1)}, u32[]{:S(2)}, u32[]{:S(2)}) collective-permute-start(bf16[2,256,128]{2,1,0:T(8,128)(2,1)S(1)} %copy_bitcast_fusion.refs_0_), channel_id=1, source_target_pairs={{0,4},{4,8},{8,12},{12,16},{16,20},{20,24},{24,28},{28,0},{1,5},{5... | collective-permute-start | bytes 393224 | tf_op jit(solution)/shard_map/ppermute | solution.py:51
  41.9 27.6 %collective-permute-start.9 = (bf16[192,1024]{1,0:T(8,128)(2,1)S(1)}, bf16[192,1024]{1,0:T(8,128)(2,1)S(1)}, u32[]{:S(2)}, u32[]{:S(2)}) collective-permute-start(bf16[192,1024]{1,0:T(8,128)(2,1)S(1)} %get-tuple-element.22), channel_id=1, source_target_pairs={{0,1},{1,2},{2,3},{3,0},{4,5},{5,6},{6,7},{7,4},{8,9},{9,10},{10,1... | collective-permute-start | bytes 1179656 | tf_op jit(solution)/shard_map/ppermute | solution.py:51
  45.1 6.0 %collective-permute-start = (bf16[2,256,128]{2,1,0:T(8,128)(2,1)S(1)}, bf16[2,256,128]{2,1,0:T(8,128)(2,1)S(1)}, u32[]{:S(2)}, u32[]{:S(2)}) collective-permute-start(bf16[2,256,128]{2,1,0:T(8,128)(2,1)S(1)} %copy_bitcast_fusion.refs_0_), channel_id=1, source_target_pairs={{0,28},{4,0},{8,4},{12,8},{16,12},{20,16},{24,20},{28,24},{1,29},{... | collective-permute-start | bytes 393224 | tf_op jit(solution)/shard_map/ppermute | solution.py:51
  48.9 14.1 %collective-permute-start.5 = (bf16[2,256,128]{2,1,0:T(8,128)(2,1)S(1)}, bf16[2,256,128]{2,1,0:T(8,128)(2,1)S(1)}, u32[]{:S(2)}, u32[]{:S(2)}) collective-permute-start(bf16[2,256,128]{2,1,0:T(8,128)(2,1)S(1)} %collective-permute-done.4.refs_7_), channel_id=1, source_target_pairs={{0,4},{4,8},{8,12},{12,16},{16,20},{20,24},{24,28},{28,0},{1,5},{5... | collective-permute-start | bytes 393224 | tf_op jit(solution)/shard_map/ppermute | solution.py:51
  51.1 13.9 %collective-permute-start.1 = (bf16[2,256,128]{2,1,0:T(8,128)(2,1)S(1)}, bf16[2,256,128]{2,1,0:T(8,128)(2,1)S(1)}, u32[]{:S(2)}, u32[]{:S(2)}) collective-permute-start(bf16[2,256,128]{2,1,0:T(8,128)(2,1)S(1)} %collective-permute-done.refs_1_), channel_id=1, source_target_pairs={{0,28},{4,0},{8,4},{12,8},{16,12},{20,16},{24,20},{28,24},{1,29},{... | collective-permute-start | bytes 393224 | tf_op jit(solution)/shard_map/ppermute | solution.py:51
  56.1 13.5 %collective-permute-start.3 = (bf16[2,256,128]{2,1,0:T(8,128)(2,1)S(1)}, bf16[2,256,128]{2,1,0:T(8,128)(2,1)S(1)}, u32[]{:S(2)}, u32[]{:S(2)}) collective-permute-start(bf16[2,256,128]{2,1,0:T(8,128)(2,1)S(1)} %copy_bitcast_fusion.refs_0_), channel_id=1, source_target_pairs={{0,16},{4,20},{8,24},{12,28},{16,0},{20,4},{24,8},{28,12},{1,17},{... | collective-permute-start | bytes 393224 | tf_op jit(solution)/shard_map/ppermute | solution.py:51
  63.1 7.9 %collective-permute-start.6 = (bf16[2,256,128]{2,1,0:T(8,128)(2,1)S(1)}, bf16[2,256,128]{2,1,0:T(8,128)(2,1)S(1)}, u32[]{:S(2)}, u32[]{:S(2)}) collective-permute-start(bf16[2,256,128]{2,1,0:T(8,128)(2,1)S(1)} %collective-permute-done.5.refs_6_), channel_id=1, source_target_pairs={{0,4},{4,8},{8,12},{12,16},{16,20},{20,24},{24,28},{28,0},{1,5},{5... | collective-permute-start | bytes 393224 | tf_op jit(solution)/shard_map/ppermute | solution.py:51
  65.0 6.5 %collective-permute-start.2 = (bf16[2,256,128]{2,1,0:T(8,128)(2,1)S(1)}, bf16[2,256,128]{2,1,0:T(8,128)(2,1)S(1)}, u32[]{:S(2)}, u32[]{:S(2)}) collective-permute-start(bf16[2,256,128]{2,1,0:T(8,128)(2,1)S(1)} %collective-permute-done.1.refs_2_), channel_id=1, source_target_pairs={{0,28},{4,0},{8,4},{12,8},{16,12},{20,16},{24,20},{28,24},{1,29},{... | collective-permute-start | bytes 393224 | tf_op jit(solution)/shard_map/ppermute | solution.py:51
  71.5 10.4 %copy-start.2 = (bf16[2,48,256]{2,1,0:T(8,128)(2,1)S(1)}, bf16[2,48,256]{2,1,0:T(8,128)(2,1)}, u32[]{:S(2)}) copy-start(bf16[2,48,256]{2,1,0:T(8,128)(2,1)} %hg.1) | copy-start | bytes 147460
  117.4 43.0 %all-to-all-start.4 = ((bf16[32,2,8,128]{3,2,1,0:T(8,128)(2,1)}), bf16[32,2,8,128]{3,2,1,0:T(8,128)(2,1)S(1)}, u32[]{:S(2)}, u32[]{:S(2)}) async-start(bf16[32,2,8,128]{3,2,1,0:T(8,128)(2,1)} %shard_map.73), calls=%async_computation.4 | async-start | bytes 262144 | tf_op jit(solution)/shard_map/all_to_all | solution.py:42
  133.2 12.3 %collective-permute-start.10 = (bf16[192,1024]{1,0:T(8,128)(2,1)S(1)}, bf16[192,1024]{1,0:T(8,128)(2,1)S(1)}, u32[]{:S(2)}, u32[]{:S(2)}) collective-permute-start(bf16[192,1024]{1,0:T(8,128)(2,1)S(1)} %get-tuple-element.28), channel_id=1, source_target_pairs={{0,3},{1,0},{2,1},{3,2},{4,7},{5,4},{6,5},{7,6},{8,11},{9,8},{10,9... | collective-permute-start | bytes 1179656 | tf_op jit(solution)/shard_map/ppermute | solution.py:51
  136.0 13.6 %collective-permute-start.11 = (bf16[192,1024]{1,0:T(8,128)(2,1)S(1)}, bf16[192,1024]{1,0:T(8,128)(2,1)S(1)}, u32[]{:S(2)}, u32[]{:S(2)}) collective-permute-start(bf16[192,1024]{1,0:T(8,128)(2,1)S(1)} %get-tuple-element.29), channel_id=1, source_target_pairs={{0,2},{1,3},{2,0},{3,1},{4,6},{5,7},{6,4},{7,5},{8,10},{9,11},{10,... | collective-permute-start | bytes 1179656 | tf_op jit(solution)/shard_map/ppermute | solution.py:51
  139.1 19.8 %collective-permute-start.12 = (bf16[192,1024]{1,0:T(8,128)(2,1)S(1)}, bf16[192,1024]{1,0:T(8,128)(2,1)S(1)}, u32[]{:S(2)}, u32[]{:S(2)}) collective-permute-start(bf16[192,1024]{1,0:T(8,128)(2,1)S(1)} %get-tuple-element.30), channel_id=1, source_target_pairs={{0,1},{1,2},{2,3},{3,0},{4,5},{5,6},{6,7},{7,4},{8,9},{9,10},{10,1... | collective-permute-start | bytes 1179656 | tf_op jit(solution)/shard_map/ppermute | solution.py:51
  158.9 1.5 copy-start.1
